TPU v7x, 32 devices: a whole 2x2x4 slice. The times are simulated.
32 devices in a mesh: ctx: 16 (over z, x, core), head: 2 (over y).
Axes of the slice: x: 2, y: 2, z: 4, core: 2. Of those that a mesh axis runs over, the one named last changes fastest.
Arguments:
- queries: bfloat16 [2, 16384, 128], P('head', 'ctx'), may hold values from -12 to 12
- key_rows: bfloat16 [2, 16384, 128], P('head', 'ctx'), may hold values from -12 to 12
- value_rows: bfloat16 [2, 16384, 128], P('head', 'ctx'), may hold values from -6 to 6
- cluster_ids: int32 [2, 16384, 1], P('head', 'ctx'), may hold values from 0 to 31; in each aligned block of 1024 rows (0 to 1023, 1024 to 2047, ..., all dimensions but the last counted through in order) at most 64 rows name the same one
- out_weight: bfloat16 [256, 2048], P(None, 'head'), may hold values from -0.375 to 0.375
Outputs:
- projected: bfloat16 [16384, 2048], P('ctx', 'head')
- centroids: float32 [2, 32, 128], P('head', 'ctx')
Inputs may be any that keep to these rules, and one draw needn't show every extreme that they name: `cluster_ids`: in each head, the 1024 tokens of one index of ctx name no cluster more than 64 times, a bound that some block reaches.
All inputs are finite; a program needn't handle non-finite values.
Results may differ from a plain program's by a relative error of at most 0.0054.
Values may be sent and summed in bfloat16 or wider, within the bound.
A program may use at most 64 MiB of HBM per device.

v0:
```python
import functools

import jax
import jax.numpy as jnp
from jax import lax
from jax.experimental import pallas as pl
from jax.experimental.pallas import tpu as pltpu
from jax.sharding import PartitionSpec as P

CL_DEV = 2
CAP = 1024
QUARTERS = 4
EMPTY = 2.0**100
LOW = -1e30

norm_eps = 1e-06
MESH = pl.DeviceIdType.MESH


def dot_t(a, b):
    return lax.dot_general(a, b, (((1,), (1,)), ((), ())), preferred_element_type=jnp.float32)


def unit_rows(values):
    return values * lax.rsqrt(jnp.mean(values * values, axis=-1, keepdims=True) + norm_eps)


def slots_of(ids, clusters, send):
    tokens = ids.shape[1]
    step = min(256, tokens)
    names = lax.broadcasted_iota(jnp.int32, (clusters, step), 0)
    before = lax.broadcasted_iota(jnp.int32, (step, step), 0)
    after = lax.broadcasted_iota(jnp.int32, (step, step), 1)
    earlier = jnp.where(before < after, 1.0, 0.0).astype(jnp.bfloat16)
    carry = jnp.zeros((clusters, 1), jnp.float32)
    out = []
    for start in range(0, tokens, step):
        part = ids[:, start : start + step]
        named = jnp.where(names == part, 1.0, 0.0)
        count = jnp.dot(named.astype(jnp.bfloat16), earlier, preferred_element_type=jnp.float32)
        rank = jnp.sum(named * (count + carry), axis=0, keepdims=True)
        carry = carry + jnp.sum(named, axis=1, keepdims=True)
        out.append(part * send + rank.astype(jnp.int32))
    return jnp.concatenate(out, axis=1)


def kernel(n, heads, send, q_hbm, k_hbm, v_hbm, ids_ref, joined_ref, cent_ref,
           rows, msg, recv, att, back, others, keys, bias, idx, cols,
           in_sem, f_send, f_recv, b_send, b_recv, h_send, h_recv, i_send, i_recv):
    tokens, width = q_hbm.shape[1], q_hbm.shape[2]
    clusters = CL_DEV * n
    part = n // QUARTERS
    block = part * send
    me = lax.axis_index("ctx")
    head = lax.axis_index("head")
    zone = me // part

    loads = []
    for i, ref in enumerate((q_hbm, k_hbm, v_hbm)):
        load = pltpu.make_async_copy(ref.at[0], rows.at[:, i * width : (i + 1) * width], in_sem.at[i])
        load.start()
        loads.append(load)

    barrier = pltpu.get_barrier_semaphore()

    def greet(i, carry):
        pl.semaphore_signal(barrier, inc=1, device_id=(lax.rem(me + i, n), head), device_id_type=MESH)
        return carry

    lax.fori_loop(1, n, greet, 0)
    for i in range(1, heads):
        pl.semaphore_signal(barrier, inc=1, device_id=(me, lax.rem(head + i, heads)), device_id_type=MESH)

    def column(slot_row):
        return jnp.transpose(jnp.broadcast_to(slot_row, (128, tokens)))

    slot_row = slots_of(ids_ref[...], clusters, send)
    cols[0] = column(slot_row)
    rows[:, 3 * width :] = jnp.ones((tokens, width), jnp.bfloat16)
    for load in loads:
        load.wait()

    place_r = lax.broadcasted_iota(jnp.int32, (block, tokens), 0)
    place_r = place_r + (place_r // send) * ((CL_DEV - 1) * send)

    def fill(j, z):
        base = (z * part * CL_DEV + j) * send
        place = jnp.where(place_r + base == slot_row, 1.0, 0.0).astype(jnp.bfloat16)
        placed = jnp.dot(place, rows[...], preferred_element_type=jnp.float32)
        held = placed[:, 3 * width :]
        new = jnp.concatenate(
            [
                placed[:, :width],
                jnp.where(held > 0.5, placed[:, width : 2 * width], EMPTY),
                placed[:, 2 * width : 3 * width],
            ],
            axis=1,
        ).astype(jnp.bfloat16)
        msg[j, pl.ds(z * part, part)] = new.reshape(part, send, 3 * width)

    def forward(j, d, source):
        return pltpu.make_async_remote_copy(
            src_ref=msg.at[j, d], dst_ref=recv.at[j, source], send_sem=f_send.at[j, d], recv_sem=f_recv.at[j, source],
            device_id=(d, head), device_id_type=MESH)

    def ship(j, z):
        def one(i, carry):
            d = z * part + lax.rem(me + i, part)

            @pl.when(d != me)
            def _():
                forward(j, d, me).start()

            return carry

        lax.fori_loop(0, part, one, 0)

    def turn(t):
        return t // QUARTERS, lax.rem(zone + QUARTERS // 2 + lax.rem(t, QUARTERS), QUARTERS)

    def told(i):
        return pltpu.make_async_remote_copy(
            src_ref=ids_ref, dst_ref=idx.at[i - 1], send_sem=i_send.at[i - 1], recv_sem=i_recv.at[i - 1],
            device_id=(me, lax.rem(head + i, heads)), device_id_type=MESH)

    fill(*turn(0))
    pl.semaphore_wait(barrier, n - 1 + heads - 1)

    def dispatch(t, carry):
        fill(*turn(t))
        ship(*turn(t - 1))
        return carry

    steps = CL_DEV * QUARTERS
    lax.fori_loop(1, steps, dispatch, 0)
    ship(*turn(steps - 1))
    for j in range(CL_DEV):
        recv[j, me] = msg[j, me]
    for i in range(1, heads):
        told(i).start()
    for i in range(1, heads):
        told(i).wait_recv()
        cols[i] = column(slots_of(idx[i - 1], clusters, send))

    def arrived(j, z):
        def one(s, carry):
            @pl.when(s != me)
            def _():
                forward(j, s, s).wait_recv()

            return carry

        lax.fori_loop(z * part, (z + 1) * part, one, 0)

    def returned(j, s, owner):
        return pltpu.make_async_remote_copy(
            src_ref=att.at[j, s], dst_ref=back.at[j, owner], send_sem=b_send.at[j, s], recv_sem=b_recv.at[j, owner],
            device_id=(s, head), device_id_type=MESH)

    tri_r = lax.broadcasted_iota(jnp.int32, (block, block), 0)
    tri_c = lax.broadcasted_iota(jnp.int32, (block, block), 1)
    causal = jnp.where(tri_c <= tri_r, 0.0, LOW)
    ones = jnp.ones((8, width), jnp.bfloat16)
    scale = jnp.float32(width ** (-0.5))

    for j in range(CL_DEV):
        sums = jnp.zeros((1, width), jnp.float32)
        for b in range(QUARTERS):
            first, last, span = b * part, (b + 1) * part, (b + 1) * block
            arrived(j, b)
            q = recv[j, first:last, :, :width].reshape(block, width)
            k32 = recv[j, first:last, :, width : 2 * width].reshape(block, width).astype(jnp.float32)
            vacant = k32 > 0.5 * EMPTY
            k32 = jnp.where(vacant, 0.0, k32)
            keys[b * block : span, :] = k32.astype(jnp.bfloat16)
            flags = dot_t(ones, jnp.where(vacant, 1.0, 0.0).astype(jnp.bfloat16))
            bias[:, b * block : span] = jnp.where(flags > 0.5, LOW, 0.0)
            scores = dot_t(q, keys[:span, :]) * scale + bias[0:1, :span]
            tail = scores[:, b * block :] + causal
            scores = tail if b == 0 else jnp.concatenate([scores[:, : b * block], tail], axis=1)
            highest = jnp.max(scores, axis=1, keepdims=True)
            weights = jnp.exp(scores - highest)
            total = jnp.sum(weights, axis=1, keepdims=True)
            v = recv[j, :last, :, 2 * width :].reshape(span, width)
            mixed = jnp.dot(weights.astype(jnp.bfloat16), v, preferred_element_type=jnp.float32)
            att[j, first:last] = (mixed / total).astype(jnp.bfloat16).reshape(part, send, width)
            unit = unit_rows(q.astype(jnp.float32)) + unit_rows(k32)
            sums = sums + jnp.sum(unit, axis=0, keepdims=True)

            def give(s, carry):
                @pl.when(s != me)
                def _():
                    returned(j, s, me).start()

                return carry

            lax.fori_loop(first, last, give, 0)
        back[j, me] = att[j, me]
        mean = jnp.mean(sums * sums, axis=-1, keepdims=True)
        cent_ref[j : j + 1, :] = sums * lax.rsqrt(mean + norm_eps)

    lanes = lax.broadcasted_iota(jnp.int32, (tokens, block), 1)
    lanes = lanes + (lanes // send) * ((CL_DEV - 1) * send)

    def gather(got, which, j, b, piece):
        column_slots = cols[which]
        wide = column_slots if block == 128 else jnp.concatenate([column_slots] * (block // 128), axis=1)
        pick = jnp.where(wide == lanes + (b * part * CL_DEV + j) * send, 1.0, 0.0).astype(jnp.bfloat16)
        return got + jnp.dot(pick, piece.reshape(block, width), preferred_element_type=jnp.float32)

    def passed(i, j, b):
        rows_of = slice(b * part, (b + 1) * part)
        return pltpu.make_async_remote_copy(
            src_ref=back.at[j, rows_of], dst_ref=others.at[i - 1, j, rows_of],
            send_sem=h_send.at[i - 1, j, b], recv_sem=h_recv.at[i - 1, j, b],
            device_id=(me, lax.rem(head + i, heads)), device_id_type=MESH)

    pieces = [(j, b) for j in range(CL_DEV) for b in range(QUARTERS)]
    got = jnp.zeros((tokens, width), jnp.float32)
    for j, b in pieces:

        def wait_back(s, carry):
            @pl.when(s != me)
            def _():
                returned(j, s, s).wait_recv()

            return carry

        lax.fori_loop(b * part, (b + 1) * part, wait_back, 0)
        for i in range(1, heads):
            passed(i, j, b).start()
        got = gather(got, 0, j, b, back[j, b * part : (b + 1) * part])
    joined_ref[:, pl.ds(pl.multiple_of(head * width, width), width)] = got.astype(jnp.bfloat16)

    for i in range(1, heads):
        got = jnp.zeros((tokens, width), jnp.float32)
        for j, b in pieces:
            passed(i, j, b).wait_recv()
            got = gather(got, i, j, b, others[i - 1, j, b * part : (b + 1) * part])
        source = lax.rem(head + heads - i, heads)
        joined_ref[:, pl.ds(pl.multiple_of(source * width, width), width)] = got.astype(jnp.bfloat16)

    def settle(i, carry):
        d = lax.rem(me + i, n)
        for j in range(CL_DEV):
            forward(j, d, me).wait_send()
            returned(j, d, me).wait_send()
        return carry

    lax.fori_loop(1, n, settle, 0)
    for i in range(1, heads):
        told(i).wait_send()
        for j, b in pieces:
            passed(i, j, b).wait_send()


def shards(n, heads, queries, key_rows, value_rows, cluster_ids, out_weight):
    tokens, width = queries.shape[1], queries.shape[2]
    send = CAP // n
    bf16, f32 = jnp.bfloat16, jnp.float32
    dma = pltpu.SemaphoreType.DMA
    joined, centroids = pl.pallas_call(
        functools.partial(kernel, n, heads, send),
        out_shape=(
            jax.ShapeDtypeStruct((tokens, heads * width), bf16),
            jax.ShapeDtypeStruct((CL_DEV, width), f32),
        ),
        in_specs=[pl.BlockSpec(memory_space=pltpu.HBM)] * 3 + [pl.BlockSpec(memory_space=pltpu.VMEM)],
        out_specs=(pl.BlockSpec(memory_space=pltpu.VMEM), pl.BlockSpec(memory_space=pltpu.VMEM)),
        scratch_shapes=[
            pltpu.VMEM((tokens, 4 * width), bf16),
            pltpu.VMEM((CL_DEV, n, send, 3 * width), bf16),
            pltpu.VMEM((CL_DEV, n, send, 3 * width), bf16),
            pltpu.VMEM((CL_DEV, n, send, width), bf16),
            pltpu.VMEM((CL_DEV, n, send, width), bf16),
            pltpu.VMEM((max(1, heads - 1), CL_DEV, n, send, width), bf16),
            pltpu.VMEM((CAP, width), bf16),
            pltpu.VMEM((8, CAP), f32),
            pltpu.VMEM((max(1, heads - 1), 1, tokens), jnp.int32),
            pltpu.VMEM((heads, tokens, 128), jnp.int32),
            dma((3,)),
            dma((CL_DEV, n)),
            dma((CL_DEV, n)),
            dma((CL_DEV, n)),
            dma((CL_DEV, n)),
            dma((max(1, heads - 1), CL_DEV, QUARTERS)),
            dma((max(1, heads - 1), CL_DEV, QUARTERS)),
            dma((max(1, heads - 1),)),
            dma((max(1, heads - 1),)),
        ],
        compiler_params=pltpu.CompilerParams(
            collective_id=0, has_side_effects=True, vmem_limit_bytes=60000000
        ),
        name="route",
    )(queries, key_rows, value_rows, cluster_ids[0, :, 0][None, :])
    projected = jnp.dot(joined, out_weight, preferred_element_type=f32).astype(bf16)
    return (projected, centroids[None])


def solution(mesh):
    in_specs = (
        P("head", "ctx", None),
        P("head", "ctx", None),
        P("head", "ctx", None),
        P("head", "ctx", None),
        P(None, "head"),
    )
    out_specs = (P("ctx", "head"), P("head", "ctx", None))
    body = functools.partial(shards, mesh.shape["ctx"], mesh.shape["head"])
    return jax.shard_map(body, mesh=mesh, in_specs=in_specs, out_specs=out_specs, check_vma=False)
```

profile of v0, /device:TPU:9, one launch (start us, length us, event | category | flops | bytes accessed | tf_op | source)
XLA Modules:
  0.0 68.4 jit_solution(9520155990003464466)
XLA Ops:
  0.6 0.0 copy-start
  0.6 64.1 %route.1 = (bf16[1024,256]{1,0:T(8,128)(2,1)}, f32[2,128]{1,0:T(2,128)}) custom-call(bf16[1,1024,128]{2,1,0:T(8,128)(2,1)} %q_hbm.1, bf16[1,1024,128]{2,1,0:T(8,128)(2,1)} %k_hbm.1, bf16[1,1024,128]{2,1,0:T(8,128)(2,1)} %v_hbm.1, s32[1,1024]{1,0:T(1,128)} %bitcast.4), custom_call_target="tpu_custom_call" | custom-call | tf_op jit(solution)/shard_map/route/pallas_call | solution.py:262
  64.7 0.0 copy-start.1
  64.7 0.0 copy-done
  64.7 3.1 %convolution_convert_fusion = bf16[1024,1024]{1,0:T(8,128)(2,1)} fusion(bf16[1024,256]{1,0:T(8,128)(2,1)} %get-tuple-element.4, bf16[256,1024]{1,0:T(8,128)(2,1)S(1)} %copy-done), kind=kOutput, calls=%fused_computation | convolution fusion | flops 537919488 | bytes 3145728 | tf_op jit(solution)/shard_map/dot_general | solution.py:296
  67.8 0.0 copy-done.1
  67.8 0.6 copy.8
Async XLA Ops:
  0.6 64.1 %copy-start = (bf16[256,1024]{1,0:T(8,128)(2,1)S(1)}, bf16[256,1024]{1,0:T(8,128)(2,1)}, u32[]{:S(2)}) copy-start(bf16[256,1024]{1,0:T(8,128)(2,1)} %param.9) | copy-start | bytes 1572868
  64.7 3.1 %copy-start.1 = (f32[2,128]{1,0:T(2,128)S(1)}, f32[2,128]{1,0:T(2,128)}, u32[]{:S(2)}) copy-start(f32[2,128]{1,0:T(2,128)} %get-tuple-element.5) | copy-start | bytes 3076
where the time goes:
time: 68.6 us; the launch traced here: 68.4 us
  Pallas kernels  64.1 us (93%)
  matrix products  3.07 us (4%)
    pallas_call x1, Pallas kernels, shards(): pl.pallas_call(functools.partial(kernel, n, heads, send), out_shape=(jax....  64.1 us
    dot_general x1, matrix products, shards(): jnp.dot(joined, out_weight, preferred_element_type=f32).astype(bf16)  3.07 us

commit v1 on v0

v1 whole, which is shorter than its diff:
```python
import functools

import jax
import jax.numpy as jnp
from jax import lax
from jax.experimental import pallas as pl
from jax.experimental.pallas import tpu as pltpu
from jax.sharding import PartitionSpec as P

CL_DEV = 2
CAP = 1024
QUARTERS = 4
CHUNKS = 4
EMPTY = 2.0**100
LOW = -1e30

norm_eps = 1e-06
MESH = pl.DeviceIdType.MESH


def dot_t(a, b):
    return lax.dot_general(a, b, (((1,), (1,)), ((), ())), preferred_element_type=jnp.float32)


def unit_rows(values):
    return values * lax.rsqrt(jnp.mean(values * values, axis=-1, keepdims=True) + norm_eps)


def slots_of(ids, clusters, send):
    tokens = ids.shape[1]
    step = min(256, tokens)
    names = lax.broadcasted_iota(jnp.int32, (clusters, step), 0)
    before = lax.broadcasted_iota(jnp.int32, (step, step), 0)
    after = lax.broadcasted_iota(jnp.int32, (step, step), 1)
    earlier = jnp.where(before < after, 1.0, 0.0).astype(jnp.bfloat16)
    carry = jnp.zeros((clusters, 1), jnp.float32)
    out = []
    for start in range(0, tokens, step):
        part = ids[:, start : start + step]
        named = jnp.where(names == part, 1.0, 0.0)
        count = jnp.dot(named.astype(jnp.bfloat16), earlier, preferred_element_type=jnp.float32)
        rank = jnp.sum(named * (count + carry), axis=0, keepdims=True)
        carry = carry + jnp.sum(named, axis=1, keepdims=True)
        out.append(part * send + rank.astype(jnp.int32))
    return jnp.concatenate(out, axis=1)


def kernel(n, heads, send, q_hbm, k_hbm, v_hbm, ids_ref, joined_ref, cent_ref,
           rows, msg, recv, asked, att, att_x, back, back_x, parts, parts_x, told, told_x, stat, stat_x,
           keys, bias, cols, held_sum, got_sum, acc,
           in_sem, f_send, f_recv, q_send, q_recv, b_send, b_recv, x_send, x_recv,
           t_send, t_recv, u_send, u_recv, h_send, h_recv, c_send, c_recv):
    tokens, width = q_hbm.shape[1], q_hbm.shape[2]
    half = n // 2
    part = n // QUARTERS
    zones = QUARTERS // 2
    block = part * send
    span = half * send
    pair = CL_DEV * send
    me = lax.axis_index("ctx")
    head = lax.axis_index("head")
    side = me // half
    pos = lax.rem(me, half)
    base = side * half
    upper = side == 1
    lower = side == 0

    loads = []
    for i, ref in enumerate((q_hbm, k_hbm, v_hbm)):
        load = pltpu.make_async_copy(ref.at[0], rows.at[:, i * width : (i + 1) * width], in_sem.at[i])
        load.start()
        loads.append(load)

    barrier = pltpu.get_barrier_semaphore()

    def greet(i, carry):
        pl.semaphore_signal(barrier, inc=1, device_id=(lax.rem(me + i, n), head), device_id_type=MESH)
        return carry

    lax.fori_loop(1, n, greet, 0)
    for i in range(1, heads):
        pl.semaphore_signal(barrier, inc=1, device_id=(me, lax.rem(head + i, heads)), device_id_type=MESH)

    slot_row = slots_of(ids_ref[...], CL_DEV * n, send)
    cols[...] = jnp.transpose(jnp.broadcast_to(slot_row, (128, tokens)))
    rows[:, 3 * width :] = jnp.ones((tokens, width), jnp.bfloat16)
    for load in loads:
        load.wait()

    place_r = lax.broadcasted_iota(jnp.int32, (block, tokens), 0)
    place_r = place_r + (place_r // send) * ((CL_DEV - 1) * send)

    def fill(j, z):
        first = (z * part * CL_DEV + j) * send
        place = jnp.where(place_r + first == slot_row, 1.0, 0.0).astype(jnp.bfloat16)
        placed = jnp.dot(place, rows[...], preferred_element_type=jnp.float32)
        held = placed[:, 3 * width :]
        new = jnp.concatenate(
            [
                placed[:, :width],
                jnp.where(held > 0.5, placed[:, width : 2 * width], EMPTY),
                placed[:, 2 * width : 3 * width],
            ],
            axis=1,
        ).astype(jnp.bfloat16)
        msg[j, pl.ds(z * part, part)] = new.reshape(part, send, 3 * width)

    def forward(j, d, source, target):
        return pltpu.make_async_remote_copy(
            src_ref=msg.at[j, d], dst_ref=recv.at[j, source], send_sem=f_send.at[j, d], recv_sem=f_recv.at[j, source],
            device_id=(target, head), device_id_type=MESH)

    def ask(j, d, source, target):
        return pltpu.make_async_remote_copy(
            src_ref=msg.at[j, d, :, pl.ds(0, width)], dst_ref=asked.at[j, source],
            send_sem=q_send.at[j, d], recv_sem=q_recv.at[j, source],
            device_id=(target, head), device_id_type=MESH)

    def ship(j, z):
        group = z // zones

        def one(i, carry):
            d = z * part + lax.rem(me + i, part)
            p = d - group * half

            @pl.when(upper)
            def _():
                ask(j, d, group * half + pos, p).start()

            @pl.when(p != pos)
            def _():
                forward(j, d, group * half + pos, base + p).start()

            return carry

        lax.fori_loop(0, part, one, 0)

    def turn(t):
        group = t // (CL_DEV * zones)
        rest = lax.rem(t, CL_DEV * zones)
        return rest // zones, group * zones + lax.rem(rest + pos // part, zones)

    fill(*turn(0))
    pl.semaphore_wait(barrier, n - 1 + heads - 1)

    def dispatch(t, carry):
        fill(*turn(t))
        ship(*turn(t - 1))
        return carry

    steps = CL_DEV * QUARTERS
    lax.fori_loop(1, steps, dispatch, 0)
    ship(*turn(steps - 1))
    for j in range(CL_DEV):
        for group in range(2):
            recv[j, group * half + pos] = msg[j, group * half + pos]

    def returned(j, s, owner, target):
        return pltpu.make_async_remote_copy(
            src_ref=att.at[j, s], dst_ref=back.at[owner, j], send_sem=b_send.at[j, s], recv_sem=b_recv.at[j, owner],
            device_id=(target, head), device_id_type=MESH)

    def answered(j, s, owner, target):
        return pltpu.make_async_remote_copy(
            src_ref=att_x.at[j, s], dst_ref=back_x.at[owner, j], send_sem=x_send.at[j, s], recv_sem=x_recv.at[j, owner],
            device_id=(target, head), device_id_type=MESH)

    def noted(s, owner, target):
        return pltpu.make_async_remote_copy(
            src_ref=told.at[s], dst_ref=stat.at[owner], send_sem=t_send.at[s], recv_sem=t_recv.at[owner],
            device_id=(target, head), device_id_type=MESH)

    def noted_x(s, owner, target):
        return pltpu.make_async_remote_copy(
            src_ref=told_x.at[s], dst_ref=stat_x.at[owner], send_sem=u_send.at[s], recv_sem=u_recv.at[owner],
            device_id=(target, head), device_id_type=MESH)

    tri_r = lax.broadcasted_iota(jnp.int32, (block, block), 0)
    tri_c = lax.broadcasted_iota(jnp.int32, (block, block), 1)
    causal = jnp.where(tri_c <= tri_r, 0.0, LOW)
    ones = jnp.ones((8, width), jnp.bfloat16)
    scale = jnp.float32(width ** (-0.5))
    lane = lax.broadcasted_iota(jnp.int32, (block, width), 1)

    def split(highest, total):
        level = highest + jnp.log(total)
        top = level.astype(jnp.bfloat16).astype(jnp.float32)
        rest = level - top
        mid = rest.astype(jnp.bfloat16).astype(jnp.float32)
        pieces = jnp.where(lane == 0, top, jnp.where(lane == 1, mid, jnp.where(lane == 2, rest - mid, 0.0)))
        return pieces.astype(jnp.bfloat16).reshape(part, send, width)

    per = 128 // pair

    def line_up(ref, out, group):
        line = dot_t(ones, ref[...].reshape(half * pair, width))
        for s in range(half):
            row = line[0:1, (s // per) * 128 : (s // per + 1) * 128]
            shift = (128 - (s % per) * pair) % 128
            out[group * half + s] = row if shift == 0 else pltpu.roll(row, shift, 1)

    def gather(picks, ref, group):
        return jnp.dot(picks, ref[group * half : (group + 1) * half].reshape(half * pair, width),
                       preferred_element_type=jnp.float32)

    chunk = tokens // CHUNKS
    slot_lane = lax.broadcasted_iota(jnp.int32, (1, half * pair), 1)

    def chosen(c, group, weight):
        column = cols[pl.ds(pl.multiple_of(c * chunk, chunk), chunk)]
        wide = jnp.concatenate([column] * (half * pair // 128), axis=1)
        return jnp.where(wide == slot_lane + group * half * pair, weight, 0.0).astype(jnp.bfloat16)

    def passed(i, c):
        at = (pl.ds(pl.multiple_of(c * chunk, chunk), chunk), pl.ds(pl.multiple_of(head * width, width), width))
        return pltpu.make_async_remote_copy(
            src_ref=joined_ref.at[at], dst_ref=joined_ref.at[at], send_sem=h_send.at[i - 1, c], recv_sem=h_recv.at[i - 1, c],
            device_id=(me, lax.rem(head + i, heads)), device_id_type=MESH)

    def lined(ref, group):
        lines = []
        for g in range(half // per):
            line = ref[group * half + g * per]
            for r in range(1, per):
                within = (lax.broadcasted_iota(jnp.int32, (1, 128), 1) // pair) == r
                line = jnp.where(within, pltpu.roll(ref[group * half + g * per + r], r * pair, 1), line)
            lines.append(line)
        return jnp.concatenate(lines, axis=1)

    def collect(group):
        def finish(c, total):
            at = pl.ds(pl.multiple_of(c * chunk, chunk), chunk)
            if group == 0:
                acc[at] = total
            else:
                joined_ref[at, pl.ds(pl.multiple_of(head * width, width), width)] = (acc[at] + total).astype(jnp.bfloat16)
                for i in range(1, heads):
                    passed(i, c).start()

        def wait_back(p, carry):
            @pl.when(p != pos)
            def _():
                for j in range(CL_DEV):
                    returned(j, group * half + p, group * half + p, base + p).wait_recv()

                @pl.when(upper)
                def _():
                    noted(group * half + p, group * half + p, base + p).wait_recv()

            @pl.when(upper)
            def _():
                for j in range(CL_DEV):
                    answered(j, group * half + p, group * half + p, p).wait_recv()
                noted_x(group * half + p, group * half + p, p).wait_recv()

            return carry

        lax.fori_loop(0, half, wait_back, 0)

        @pl.when(lower)
        def _():
            def step(c, carry):
                finish(c, gather(chosen(c, group, 1.0), back, group))
                return carry

            lax.fori_loop(0, CHUNKS, step, 0)

        @pl.when(upper)
        def _():
            ours, theirs = lined(stat, group), lined(stat_x, group)
            keep = 1.0 / (1.0 + jnp.exp(theirs - ours))
            add = 1.0 / (1.0 + jnp.exp(ours - theirs))

            def step(c, carry):
                finish(c, gather(chosen(c, group, keep), back, group) + gather(chosen(c, group, add), back_x, group))
                return carry

            lax.fori_loop(0, CHUNKS, step, 0)

    for group in range(2):
        for j in range(CL_DEV):
            sums = jnp.zeros((1, width), jnp.float32)
            for b in range(zones):
                first, last, far = group * half + b * part, group * half + (b + 1) * part, (b + 1) * block

                def arrived(s, carry):
                    @pl.when(s != group * half + pos)
                    def _():
                        forward(j, s, s, base + s - group * half).wait_recv()

                    return carry

                lax.fori_loop(first, last, arrived, 0)
                q = recv[j, first:last, :, :width].reshape(block, width)
                k32 = recv[j, first:last, :, width : 2 * width].reshape(block, width).astype(jnp.float32)
                vacant = k32 > 0.5 * EMPTY
                k32 = jnp.where(vacant, 0.0, k32)
                keys[b * block : far, :] = k32.astype(jnp.bfloat16)
                flags = dot_t(ones, jnp.where(vacant, 1.0, 0.0).astype(jnp.bfloat16))
                bias[:, b * block : far] = jnp.where(flags > 0.5, LOW, 0.0)
                scores = dot_t(q, keys[:far, :]) * scale + bias[0:1, :far]
                tail = scores[:, b * block :] + causal
                scores = tail if b == 0 else jnp.concatenate([scores[:, : b * block], tail], axis=1)
                highest = jnp.max(scores, axis=1, keepdims=True)
                weights = jnp.exp(scores - highest)
                total = jnp.sum(weights, axis=1, keepdims=True)
                v = recv[j, group * half : last, :, 2 * width :].reshape(far, width)
                mixed = jnp.dot(weights.astype(jnp.bfloat16), v, preferred_element_type=jnp.float32)
                att[j, first:last] = (mixed / total).astype(jnp.bfloat16).reshape(part, send, width)
                parts[b * part : (b + 1) * part, j] = split(highest, total)
                unit = unit_rows(q.astype(jnp.float32)) + unit_rows(k32)
                sums = sums + jnp.sum(unit, axis=0, keepdims=True)

                def give(s, carry):
                    @pl.when(s != group * half + pos)
                    def _():
                        returned(j, s, group * half + pos, base + s - group * half).start()

                    return carry

                lax.fori_loop(first, last, give, 0)
            back[group * half + pos, j] = att[j, group * half + pos]
            held_sum[group, j : j + 1, :] = sums

            @pl.when(lower)
            def _():
                for b in range(zones):
                    first, last = group * half + b * part, group * half + (b + 1) * part

                    def wait_ask(s, carry):
                        ask(j, s, s, half + s - group * half).wait_recv()
                        return carry

                    lax.fori_loop(first, last, wait_ask, 0)
                    q = asked[j, first:last].reshape(block, width)
                    scores = dot_t(q, keys[...]) * scale + bias[0:1, :]
                    highest = jnp.max(scores, axis=1, keepdims=True)
                    weights = jnp.exp(scores - highest)
                    total = jnp.sum(weights, axis=1, keepdims=True)
                    v = recv[j, group * half : (group + 1) * half, :, 2 * width :].reshape(span, width)
                    mixed = jnp.dot(weights.astype(jnp.bfloat16), v, preferred_element_type=jnp.float32)
                    att_x[j, first:last] = (mixed / total).astype(jnp.bfloat16).reshape(part, send, width)
                    parts_x[b * part : (b + 1) * part, j] = split(highest, total)

                    def give_x(s, carry):
                        answered(j, s, group * half + pos, half + s - group * half).start()
                        return carry

                    lax.fori_loop(first, last, give_x, 0)

        @pl.when(upper)
        def _():
            line_up(parts, told, group)

            def tell(s, carry):
                @pl.when(s != pos)
                def _():
                    noted(group * half + s, group * half + pos, half + s).start()

                return carry

            lax.fori_loop(0, half, tell, 0)
            stat[group * half + pos] = told[group * half + pos]

        @pl.when(lower)
        def _():
            line_up(parts_x, told_x, group)

            def tell(s, carry):
                noted_x(group * half + s, group * half + pos, half + s).start()
                return carry

            lax.fori_loop(0, half, tell, 0)

    other = 1 - side
    swap = pltpu.make_async_remote_copy(
        src_ref=held_sum.at[other], dst_ref=got_sum, send_sem=c_send, recv_sem=c_recv,
        device_id=(other * half + pos, head), device_id_type=MESH)
    swap.start()

    collect(0)
    collect(1)

    swap.wait()
    sums = held_sum[side] + got_sum[...]
    mean = jnp.mean(sums * sums, axis=-1, keepdims=True)
    cent_ref[...] = sums * lax.rsqrt(mean + norm_eps)

    for i in range(1, heads):
        for c in range(CHUNKS):
            passed(i, c).wait()

    def settle(p, carry):
        for group in range(2):
            d = group * half + p

            @pl.when(p != pos)
            def _():
                for j in range(CL_DEV):
                    forward(j, d, group * half + pos, base + p).wait_send()
                    returned(j, d, group * half + pos, base + p).wait_send()

                @pl.when(upper)
                def _():
                    noted(d, group * half + pos, base + p).wait_send()

            @pl.when(upper)
            def _():
                for j in range(CL_DEV):
                    ask(j, d, group * half + pos, p).wait_send()

            @pl.when(lower)
            def _():
                for j in range(CL_DEV):
                    answered(j, d, group * half + pos, half + p).wait_send()
                noted_x(d, group * half + pos, half + p).wait_send()

        return carry

    lax.fori_loop(0, half, settle, 0)


def shards(n, heads, queries, key_rows, value_rows, cluster_ids, out_weight):
    tokens, width = queries.shape[1], queries.shape[2]
    send = CAP // n
    half = n // 2
    bf16, f32 = jnp.bfloat16, jnp.float32
    dma = pltpu.SemaphoreType.DMA
    joined, centroids = pl.pallas_call(
        functools.partial(kernel, n, heads, send),
        out_shape=(
            jax.ShapeDtypeStruct((tokens, heads * width), bf16),
            jax.ShapeDtypeStruct((CL_DEV, width), f32),
        ),
        in_specs=[pl.BlockSpec(memory_space=pltpu.HBM)] * 3 + [pl.BlockSpec(memory_space=pltpu.VMEM)],
        out_specs=(pl.BlockSpec(memory_space=pltpu.VMEM), pl.BlockSpec(memory_space=pltpu.VMEM)),
        scratch_shapes=[
            pltpu.VMEM((tokens, 4 * width), bf16),
            pltpu.VMEM((CL_DEV, n, send, 3 * width), bf16),
            pltpu.VMEM((CL_DEV, n, send, 3 * width), bf16),
            pltpu.VMEM((CL_DEV, n, send, width), bf16),
            pltpu.VMEM((CL_DEV, n, send, width), bf16),
            pltpu.VMEM((CL_DEV, n, send, width), bf16),
            pltpu.VMEM((n, CL_DEV, send, width), bf16),
            pltpu.VMEM((n, CL_DEV, send, width), bf16),
            pltpu.VMEM((half, CL_DEV, send, width), bf16),
            pltpu.VMEM((half, CL_DEV, send, width), bf16),
            pltpu.VMEM((n, 1, 128), f32),
            pltpu.VMEM((n, 1, 128), f32),
            pltpu.VMEM((n, 1, 128), f32),
            pltpu.VMEM((n, 1, 128), f32),
            pltpu.VMEM((half * send, width), bf16),
            pltpu.VMEM((8, half * send), f32),
            pltpu.VMEM((tokens, 128), jnp.int32),
            pltpu.VMEM((2, CL_DEV, width), f32),
            pltpu.VMEM((CL_DEV, width), f32),
            pltpu.VMEM((tokens, width), f32),
            dma((3,)),
        ]
        + [dma((CL_DEV, n))] * 8
        + [dma((n,))] * 4
        + [dma((max(1, heads - 1), CHUNKS))] * 2
        + [dma, dma],
        compiler_params=pltpu.CompilerParams(
            collective_id=0, has_side_effects=True, vmem_limit_bytes=60000000
        ),
        name="route",
    )(queries, key_rows, value_rows, cluster_ids[0, :, 0][None, :])
    projected = jnp.dot(joined, out_weight, preferred_element_type=f32).astype(bf16)
    return (projected, centroids[None])


def solution(mesh):
    in_specs = (
        P("head", "ctx", None),
        P("head", "ctx", None),
        P("head", "ctx", None),
        P("head", "ctx", None),
        P(None, "head"),
    )
    out_specs = (P("ctx", "head"), P("head", "ctx", None))
    body = functools.partial(shards, mesh.shape["ctx"], mesh.shape["head"])
    return jax.shard_map(body, mesh=mesh, in_specs=in_specs, out_specs=out_specs, check_vma=False)
```

time: 68.6 us -> 60.3 us (0.88)
  the two profiles are of different devices: /device:TPU:9 before, /device:TPU:16 now
where the time goes in v1:
time: 60.3 us; the launch traced here: 60.1 us
  Pallas kernels  55.8 us (93%)
  matrix products  3.07 us (5%)
  between operations  0.66 us (1%)
    pallas_call x1, Pallas kernels, shards(): pl.pallas_call(functools.partial(kernel, n, heads, send), out_shape=(jax....  55.8 us
    dot_general x1, matrix products, shards(): jnp.dot(joined, out_weight, preferred_element_type=f32).astype(bf16)  3.07 us

profile of v1, /device:TPU:16, one launch (start us, length us, event | category | flops | bytes accessed | tf_op | source)
XLA Modules:
  0.0 60.1 jit_solution(11146298007354565584)
XLA Ops:
  0.6 0.0 copy-start
  0.6 55.8 %route.1 = (bf16[1024,256]{1,0:T(8,128)(2,1)}, f32[2,128]{1,0:T(2,128)}) custom-call(bf16[1,1024,128]{2,1,0:T(8,128)(2,1)} %q_hbm.1, bf16[1,1024,128]{2,1,0:T(8,128)(2,1)} %k_hbm.1, bf16[1,1024,128]{2,1,0:T(8,128)(2,1)} %v_hbm.1, s32[1,1024]{1,0:T(1,128)} %bitcast.4), custom_call_target="tpu_custom_call" | custom-call | tf_op jit(solution)/shard_map/route/pallas_call | solution.py:429
  56.5 0.0 copy-start.1
  56.5 0.0 copy-done
  56.5 3.1 %convolution_convert_fusion = bf16[1024,1024]{1,0:T(8,128)(2,1)} fusion(bf16[1024,256]{1,0:T(8,128)(2,1)} %get-tuple-element.4, bf16[256,1024]{1,0:T(8,128)(2,1)S(1)} %copy-done), kind=kOutput, calls=%fused_computation | convolution fusion | flops 537919488 | bytes 3145728 | tf_op jit(solution)/shard_map/dot_general | solution.py:469
  59.5 0.0 copy-done.1
  59.5 0.6 copy.8
Async XLA Ops:
  0.6 55.8 %copy-start = (bf16[256,1024]{1,0:T(8,128)(2,1)S(1)}, bf16[256,1024]{1,0:T(8,128)(2,1)}, u32[]{:S(2)}) copy-start(bf16[256,1024]{1,0:T(8,128)(2,1)} %param.9) | copy-start | bytes 1572868
  56.5 3.1 %copy-start.1 = (f32[2,128]{1,0:T(2,128)S(1)}, f32[2,128]{1,0:T(2,128)}, u32[]{:S(2)}) copy-start(f32[2,128]{1,0:T(2,128)} %get-tuple-element.5) | copy-start | bytes 3076

commit v2 on v1

--- a/solution.py
+++ b/solution.py
@@ -45,8 +45,8 @@
     return jnp.concatenate(out, axis=1)
 
 
-def kernel(n, heads, send, q_hbm, k_hbm, v_hbm, ids_ref, joined_ref, cent_ref,
-           rows, msg, recv, asked, att, att_x, back, back_x, parts, parts_x, told, told_x, stat, stat_x,
+def kernel(n, heads, send, q_hbm, k_hbm, v_hbm, ids_hbm, weight_hbm, joined_ref, sums_ref, weight_ref,
+           ids_ref, rows, msg, recv, asked, att, att_x, back, back_x, parts, parts_x, told, told_x, stat, stat_x,
            keys, bias, cols, held_sum, got_sum, acc,
            in_sem, f_send, f_recv, q_send, q_recv, b_send, b_recv, x_send, x_recv,
            t_send, t_recv, u_send, u_recv, h_send, h_recv, c_send, c_recv):
@@ -65,12 +65,17 @@
     upper = side == 1
     lower = side == 0
 
+    named = pltpu.make_async_copy(ids_hbm, ids_ref, in_sem.at[3])
+    named.start()
     loads = []
     for i, ref in enumerate((q_hbm, k_hbm, v_hbm)):
         load = pltpu.make_async_copy(ref.at[0], rows.at[:, i * width : (i + 1) * width], in_sem.at[i])
         load.start()
         loads.append(load)
 
+    keep_weight = pltpu.make_async_copy(weight_hbm, weight_ref, in_sem.at[4])
+    keep_weight.start()
+
     barrier = pltpu.get_barrier_semaphore()
 
     def greet(i, carry):
@@ -81,8 +86,8 @@
     for i in range(1, heads):
         pl.semaphore_signal(barrier, inc=1, device_id=(me, lax.rem(head + i, heads)), device_id_type=MESH)
 
+    named.wait()
     slot_row = slots_of(ids_ref[...], CL_DEV * n, send)
-    cols[...] = jnp.transpose(jnp.broadcast_to(slot_row, (128, tokens)))
     rows[:, 3 * width :] = jnp.ones((tokens, width), jnp.bfloat16)
     for load in loads:
         load.wait()
@@ -142,15 +147,15 @@
 
     fill(*turn(0))
     pl.semaphore_wait(barrier, n - 1 + heads - 1)
+    ship(*turn(0))
 
     def dispatch(t, carry):
         fill(*turn(t))
-        ship(*turn(t - 1))
+        ship(*turn(t))
         return carry
 
-    steps = CL_DEV * QUARTERS
-    lax.fori_loop(1, steps, dispatch, 0)
-    ship(*turn(steps - 1))
+    lax.fori_loop(1, CL_DEV * QUARTERS, dispatch, 0)
+    cols[...] = jnp.transpose(jnp.broadcast_to(slot_row, (128, tokens)))
     for j in range(CL_DEV):
         for group in range(2):
             recv[j, group * half + pos] = msg[j, group * half + pos]
@@ -383,8 +388,8 @@
 
     swap.wait()
     sums = held_sum[side] + got_sum[...]
-    mean = jnp.mean(sums * sums, axis=-1, keepdims=True)
-    cent_ref[...] = sums * lax.rsqrt(mean + norm_eps)
+    sums_ref[...] = sums
+    keep_weight.wait()
 
     for i in range(1, heads):
         for c in range(CHUNKS):
@@ -418,6 +423,38 @@
         return carry
 
     lax.fori_loop(0, half, settle, 0)
+
+
+def project_kernel(steps, joined_ref, weight_ref, sums_ref, out_hbm, cent_ref, out, sem):
+    rows = joined_ref.shape[0] // steps
+    copies = []
+    for i in range(steps):
+        at = slice(i * rows, (i + 1) * rows)
+        out[at] = jnp.dot(joined_ref[at], weight_ref[...], preferred_element_type=jnp.float32).astype(jnp.bfloat16)
+        copy = pltpu.make_async_copy(out.at[at], out_hbm.at[at], sem.at[i])
+        copy.start()
+        copies.append(copy)
+    sums = sums_ref[...]
+    mean = jnp.mean(sums * sums, axis=-1, keepdims=True)
+    cent_ref[0] = sums * lax.rsqrt(mean + norm_eps)
+    for copy in copies:
+        copy.wait()
+
+
+def project(joined, weight, sums, steps):
+    tokens, columns = joined.shape[0], weight.shape[1]
+    return pl.pallas_call(
+        functools.partial(project_kernel, steps),
+        out_shape=(
+            jax.ShapeDtypeStruct((tokens, columns), jnp.bfloat16),
+            jax.ShapeDtypeStruct((1,) + sums.shape, jnp.float32),
+        ),
+        in_specs=[pl.BlockSpec(memory_space=pltpu.VMEM)] * 3,
+        out_specs=(pl.BlockSpec(memory_space=pltpu.HBM), pl.BlockSpec(memory_space=pltpu.VMEM)),
+        scratch_shapes=[pltpu.VMEM((tokens, columns), jnp.bfloat16), pltpu.SemaphoreType.DMA((steps,))],
+        compiler_params=pltpu.CompilerParams(vmem_limit_bytes=8000000),
+        name="project",
+    )(joined, weight, sums)
 
 
 def shards(n, heads, queries, key_rows, value_rows, cluster_ids, out_weight):
@@ -426,15 +463,19 @@
     half = n // 2
     bf16, f32 = jnp.bfloat16, jnp.float32
     dma = pltpu.SemaphoreType.DMA
-    joined, centroids = pl.pallas_call(
+    pinned = [pltpu.with_memory_space_constraint(x, pltpu.HBM)
+              for x in (queries, key_rows, value_rows, cluster_ids[0, :, 0][None, :], out_weight)]
+    joined, sums, weight = pl.pallas_call(
         functools.partial(kernel, n, heads, send),
         out_shape=(
             jax.ShapeDtypeStruct((tokens, heads * width), bf16),
             jax.ShapeDtypeStruct((CL_DEV, width), f32),
+            jax.ShapeDtypeStruct(out_weight.shape, bf16),
         ),
-        in_specs=[pl.BlockSpec(memory_space=pltpu.HBM)] * 3 + [pl.BlockSpec(memory_space=pltpu.VMEM)],
-        out_specs=(pl.BlockSpec(memory_space=pltpu.VMEM), pl.BlockSpec(memory_space=pltpu.VMEM)),
+        in_specs=[pl.BlockSpec(memory_space=pltpu.HBM)] * 5,
+        out_specs=(pl.BlockSpec(memory_space=pltpu.VMEM),) * 3,
         scratch_shapes=[
+            pltpu.VMEM((1, tokens), jnp.int32),
             pltpu.VMEM((tokens, 4 * width), bf16),
             pltpu.VMEM((CL_DEV, n, send, 3 * width), bf16),
             pltpu.VMEM((CL_DEV, n, send, 3 * width), bf16),
@@ -455,19 +496,18 @@
             pltpu.VMEM((2, CL_DEV, width), f32),
             pltpu.VMEM((CL_DEV, width), f32),
             pltpu.VMEM((tokens, width), f32),
-            dma((3,)),
+            dma((5,)),
         ]
         + [dma((CL_DEV, n))] * 8
         + [dma((n,))] * 4
         + [dma((max(1, heads - 1), CHUNKS))] * 2
         + [dma, dma],
         compiler_params=pltpu.CompilerParams(
-            collective_id=0, has_side_effects=True, vmem_limit_bytes=60000000
+            collective_id=0, has_side_effects=True, vmem_limit_bytes=40000000
         ),
         name="route",
-    )(queries, key_rows, value_rows, cluster_ids[0, :, 0][None, :])
-    projected = jnp.dot(joined, out_weight, preferred_element_type=f32).astype(bf16)
-    return (projected, centroids[None])
+    )(*pinned)
+    return project(joined, weight, sums, 4)
 
 
 def solution(mesh):

time: 60.3 us -> 57.2 us (0.949)
  matrix products: 3.07 us -> 0 us
    dot_general x1 -> x0, matrix products: 3.07 us -> none  [shards(): jnp.dot(joined, out_weight, preferred_element_type=f32).astype(bf16)]
    pallas_call x0 -> x1, Pallas kernels: none -> 2.22 us  [project(): pl.pallas_call(functools.partial(project_kernel, steps), out_shape=(jax.S...]
    pallas_call x1, Pallas kernels: 55.8 us -> 54.2 us  [shards(): pl.pallas_call(functools.partial(kernel, n, heads, send), out_shape=(jax....]
where the time goes in v2:
time: 57.2 us; the launch traced here: 57 us
  Pallas kernels  56.4 us (99%)
  between operations  0.64 us (1%)
    pallas_call x1, Pallas kernels, shards(): pl.pallas_call(functools.partial(kernel, n, heads, send), out_shape=(jax....  54.2 us
    pallas_call x1, Pallas kernels, project(): pl.pallas_call(functools.partial(project_kernel, steps), out_shape=(jax.S...  2.22 us

profile of v2, /device:TPU:16, one launch (start us, length us, event | category | flops | bytes accessed | tf_op | source)
XLA Modules:
  0.0 57.0 jit_solution(12561083863745050931)
XLA Ops:
  0.6 54.2 %route.1 = (bf16[1024,256]{1,0:T(8,128)(2,1)S(1)}, f32[2,128]{1,0:T(2,128)S(1)}, bf16[256,1024]{1,0:T(8,128)(2,1)S(1)}) custom-call(bf16[1,1024,128]{2,1,0:T(8,128)(2,1)} %q_hbm.1, bf16[1,1024,128]{2,1,0:T(8,128)(2,1)} %k_hbm.1, bf16[1,1024,128]{2,1,0:T(8,128)(2,1)} %v_hbm.1, s32[1,1024]{1,0:T(1,128)} %bitcast.1, bf16[256,1024]{1,0:T(8,128)(2,1)} %weight_hbm.1), custom_call_target="tpu_custom_call" | custom-call | tf_op jit(solution)/shard_map/route/pallas_call | solution.py:468
  54.8 2.2 %project.1 = (bf16[1024,1024]{1,0:T(8,128)(2,1)}, f32[1,2,128]{2,1,0:T(2,128)}) custom-call(bf16[1024,256]{1,0:T(8,128)(2,1)S(1)} %get-tuple-element.5.joined_ref, bf16[256,1024]{1,0:T(8,128)(2,1)S(1)} %get-tuple-element.6.weight_ref, f32[2,128]{1,0:T(2,128)S(1)} %get-tuple-element.7.sums_ref), custom_call_target="tpu_custom_call" | custom-call | tf_op jit(solution)/shard_map/project/pallas_call | solution.py:446

commit v3 on v2

--- a/solution.py
+++ b/solution.py
@@ -100,15 +100,13 @@
         place = jnp.where(place_r + first == slot_row, 1.0, 0.0).astype(jnp.bfloat16)
         placed = jnp.dot(place, rows[...], preferred_element_type=jnp.float32)
         held = placed[:, 3 * width :]
-        new = jnp.concatenate(
-            [
-                placed[:, :width],
-                jnp.where(held > 0.5, placed[:, width : 2 * width], EMPTY),
-                placed[:, 2 * width : 3 * width],
-            ],
-            axis=1,
-        ).astype(jnp.bfloat16)
-        msg[j, pl.ds(z * part, part)] = new.reshape(part, send, 3 * width)
+        pieces = (
+            placed[:, :width],
+            jnp.where(held > 0.5, placed[:, width : 2 * width], EMPTY),
+            placed[:, 2 * width : 3 * width],
+        )
+        for i, piece in enumerate(pieces):
+            msg[j, pl.ds(z * part, part), i] = piece.astype(jnp.bfloat16).reshape(part, send, width)
 
     def forward(j, d, source, target):
         return pltpu.make_async_remote_copy(
@@ -117,7 +115,7 @@
 
     def ask(j, d, source, target):
         return pltpu.make_async_remote_copy(
-            src_ref=msg.at[j, d, :, pl.ds(0, width)], dst_ref=asked.at[j, source],
+            src_ref=msg.at[j, d, 0], dst_ref=asked.at[j, source],
             send_sem=q_send.at[j, d], recv_sem=q_recv.at[j, source],
             device_id=(target, head), device_id_type=MESH)
 
@@ -143,7 +141,7 @@
     def turn(t):
         group = t // (CL_DEV * zones)
         rest = lax.rem(t, CL_DEV * zones)
-        return rest // zones, group * zones + lax.rem(rest + pos // part, zones)
+        return rest // zones, group * zones + lax.rem(rest + 1 + pos // part, zones)
 
     fill(*turn(0))
     pl.semaphore_wait(barrier, n - 1 + heads - 1)
@@ -296,8 +294,8 @@
                     return carry
 
                 lax.fori_loop(first, last, arrived, 0)
-                q = recv[j, first:last, :, :width].reshape(block, width)
-                k32 = recv[j, first:last, :, width : 2 * width].reshape(block, width).astype(jnp.float32)
+                q = recv[j, first:last, 0].reshape(block, width)
+                k32 = recv[j, first:last, 1].reshape(block, width).astype(jnp.float32)
                 vacant = k32 > 0.5 * EMPTY
                 k32 = jnp.where(vacant, 0.0, k32)
                 keys[b * block : far, :] = k32.astype(jnp.bfloat16)
@@ -309,7 +307,7 @@
                 highest = jnp.max(scores, axis=1, keepdims=True)
                 weights = jnp.exp(scores - highest)
                 total = jnp.sum(weights, axis=1, keepdims=True)
-                v = recv[j, group * half : last, :, 2 * width :].reshape(far, width)
+                v = recv[j, group * half : last, 2].reshape(far, width)
                 mixed = jnp.dot(weights.astype(jnp.bfloat16), v, preferred_element_type=jnp.float32)
                 att[j, first:last] = (mixed / total).astype(jnp.bfloat16).reshape(part, send, width)
                 parts[b * part : (b + 1) * part, j] = split(highest, total)
@@ -342,7 +340,7 @@
                     highest = jnp.max(scores, axis=1, keepdims=True)
                     weights = jnp.exp(scores - highest)
                     total = jnp.sum(weights, axis=1, keepdims=True)
-                    v = recv[j, group * half : (group + 1) * half, :, 2 * width :].reshape(span, width)
+                    v = recv[j, group * half : (group + 1) * half, 2].reshape(span, width)
                     mixed = jnp.dot(weights.astype(jnp.bfloat16), v, preferred_element_type=jnp.float32)
                     att_x[j, first:last] = (mixed / total).astype(jnp.bfloat16).reshape(part, send, width)
                     parts_x[b * part : (b + 1) * part, j] = split(highest, total)
@@ -425,18 +423,19 @@
     lax.fori_loop(0, half, settle, 0)
 
 
-def project_kernel(steps, joined_ref, weight_ref, sums_ref, out_hbm, cent_ref, out, sem):
+def project_kernel(steps, joined_ref, weight_ref, sums_ref, out_hbm, cent_hbm, out, cent, sem):
     rows = joined_ref.shape[0] // steps
-    copies = []
+    sums = sums_ref[...]
+    mean = jnp.mean(sums * sums, axis=-1, keepdims=True)
+    cent[0] = sums * lax.rsqrt(mean + norm_eps)
+    copies = [pltpu.make_async_copy(cent, cent_hbm, sem.at[steps])]
+    copies[0].start()
     for i in range(steps):
         at = slice(i * rows, (i + 1) * rows)
         out[at] = jnp.dot(joined_ref[at], weight_ref[...], preferred_element_type=jnp.float32).astype(jnp.bfloat16)
         copy = pltpu.make_async_copy(out.at[at], out_hbm.at[at], sem.at[i])
         copy.start()
         copies.append(copy)
-    sums = sums_ref[...]
-    mean = jnp.mean(sums * sums, axis=-1, keepdims=True)
-    cent_ref[0] = sums * lax.rsqrt(mean + norm_eps)
     for copy in copies:
         copy.wait()
 
@@ -450,8 +449,12 @@
             jax.ShapeDtypeStruct((1,) + sums.shape, jnp.float32),
         ),
         in_specs=[pl.BlockSpec(memory_space=pltpu.VMEM)] * 3,
-        out_specs=(pl.BlockSpec(memory_space=pltpu.HBM), pl.BlockSpec(memory_space=pltpu.VMEM)),
-        scratch_shapes=[pltpu.VMEM((tokens, columns), jnp.bfloat16), pltpu.SemaphoreType.DMA((steps,))],
+        out_specs=(pl.BlockSpec(memory_space=pltpu.HBM),) * 2,
+        scratch_shapes=[
+            pltpu.VMEM((tokens, columns), jnp.bfloat16),
+            pltpu.VMEM((1,) + sums.shape, jnp.float32),
+            pltpu.SemaphoreType.DMA((steps + 1,)),
+        ],
         compiler_params=pltpu.CompilerParams(vmem_limit_bytes=8000000),
         name="project",
     )(joined, weight, sums)
@@ -477,8 +480,8 @@
         scratch_shapes=[
             pltpu.VMEM((1, tokens), jnp.int32),
             pltpu.VMEM((tokens, 4 * width), bf16),
-            pltpu.VMEM((CL_DEV, n, send, 3 * width), bf16),
-            pltpu.VMEM((CL_DEV, n, send, 3 * width), bf16),
+            pltpu.VMEM((CL_DEV, n, 3, send, width), bf16),
+            pltpu.VMEM((CL_DEV, n, 3, send, width), bf16),
             pltpu.VMEM((CL_DEV, n, send, width), bf16),
             pltpu.VMEM((CL_DEV, n, send, width), bf16),
             pltpu.VMEM((CL_DEV, n, send, width), bf16),

time: 57.2 us -> 56.8 us (level)
  no operation moved by 1% of the time
where the time goes in v3:
time: 56.8 us; the launch traced here: 56.6 us
  Pallas kernels  55.9 us (98%)
  between operations  0.64 us (1%)
    pallas_call x1, Pallas kernels, shards(): pl.pallas_call(functools.partial(kernel, n, heads, send), out_shape=(jax....  54.3 us
    pallas_call x1, Pallas kernels, project(): pl.pallas_call(functools.partial(project_kernel, steps), out_shape=(jax.S...  1.67 us

profile of v3, /device:TPU:16, one launch (start us, length us, event | category | flops | bytes accessed | tf_op | source)
XLA Modules:
  0.0 56.6 jit_solution(4905778359753954334)
XLA Ops:
  0.6 54.3 %route.1 = (bf16[1024,256]{1,0:T(8,128)(2,1)S(1)}, f32[2,128]{1,0:T(2,128)S(1)}, bf16[256,1024]{1,0:T(8,128)(2,1)S(1)}) custom-call(bf16[1,1024,128]{2,1,0:T(8,128)(2,1)} %q_hbm.1, bf16[1,1024,128]{2,1,0:T(8,128)(2,1)} %k_hbm.1, bf16[1,1024,128]{2,1,0:T(8,128)(2,1)} %v_hbm.1, s32[1,1024]{1,0:T(1,128)} %bitcast.1, bf16[256,1024]{1,0:T(8,128)(2,1)} %weight_hbm.1), custom_call_target="tpu_custom_call" | custom-call | tf_op jit(solution)/shard_map/route/pallas_call | solution.py:471
  54.9 1.7 %project.1 = (bf16[1024,1024]{1,0:T(8,128)(2,1)}, f32[1,2,128]{2,1,0:T(2,128)}) custom-call(bf16[1024,256]{1,0:T(8,128)(2,1)S(1)} %get-tuple-element.5.joined_ref, bf16[256,1024]{1,0:T(8,128)(2,1)S(1)} %get-tuple-element.6.weight_ref, f32[2,128]{1,0:T(2,128)S(1)} %get-tuple-element.7.sums_ref), custom_call_target="tpu_custom_call" | custom-call | tf_op jit(solution)/shard_map/project/pallas_call | solution.py:445

commit v4 on v3

--- a/solution.py
+++ b/solution.py
@@ -47,7 +47,7 @@
 
 def kernel(n, heads, send, q_hbm, k_hbm, v_hbm, ids_hbm, weight_hbm, joined_ref, sums_ref, weight_ref,
            ids_ref, rows, msg, recv, asked, att, att_x, back, back_x, parts, parts_x, told, told_x, stat, stat_x,
-           keys, bias, cols, held_sum, got_sum, acc,
+           lent, keys, bias, keys_x, bias_x, cols, held_sum, got_sum, acc,
            in_sem, f_send, f_recv, q_send, q_recv, b_send, b_recv, x_send, x_recv,
            t_send, t_recv, u_send, u_recv, h_send, h_recv, c_send, c_recv):
     tokens, width = q_hbm.shape[1], q_hbm.shape[2]
@@ -119,16 +119,27 @@
             send_sem=q_send.at[j, d], recv_sem=q_recv.at[j, source],
             device_id=(target, head), device_id_type=MESH)
 
+    def lend(d, source, target):
+        return pltpu.make_async_remote_copy(
+            src_ref=msg.at[CL_DEV - 1, d, pl.ds(1, 2)], dst_ref=lent.at[source],
+            send_sem=q_send.at[CL_DEV - 1, d], recv_sem=q_recv.at[CL_DEV - 1, half + source],
+            device_id=(target, head), device_id_type=MESH)
+
     def ship(j, z):
         group = z // zones
+        final = jnp.logical_and(group == 1, j == CL_DEV - 1)
 
         def one(i, carry):
             d = z * part + lax.rem(me + i, part)
             p = d - group * half
 
-            @pl.when(upper)
+            @pl.when(jnp.logical_and(upper, jnp.logical_not(final)))
             def _():
                 ask(j, d, group * half + pos, p).start()
+
+            @pl.when(jnp.logical_and(lower, final))
+            def _():
+                lend(d, pos, half + p).start()
 
             @pl.when(p != pos)
             def _():
@@ -154,6 +165,7 @@
 
     lax.fori_loop(1, CL_DEV * QUARTERS, dispatch, 0)
     cols[...] = jnp.transpose(jnp.broadcast_to(slot_row, (128, tokens)))
+    back_x[half:, CL_DEV - 1] = jnp.zeros((half, send, width), jnp.bfloat16)
     for j in range(CL_DEV):
         for group in range(2):
             recv[j, group * half + pos] = msg[j, group * half + pos]
@@ -252,7 +264,7 @@
 
             @pl.when(upper)
             def _():
-                for j in range(CL_DEV):
+                for j in range(CL_DEV - group):
                     answered(j, group * half + p, group * half + p, p).wait_recv()
                 noted_x(group * half + p, group * half + p, p).wait_recv()
 
@@ -273,6 +285,9 @@
             ours, theirs = lined(stat, group), lined(stat_x, group)
             keep = 1.0 / (1.0 + jnp.exp(theirs - ours))
             add = 1.0 / (1.0 + jnp.exp(ours - theirs))
+            if group == 1:
+                whole = (slot_lane // send) % CL_DEV == CL_DEV - 1
+                keep, add = jnp.where(whole, 1.0, keep), jnp.where(whole, 0.0, add)
 
             def step(c, carry):
                 finish(c, gather(chosen(c, group, keep), back, group) + gather(chosen(c, group, add), back_x, group))
@@ -283,6 +298,22 @@
     for group in range(2):
         for j in range(CL_DEV):
             sums = jnp.zeros((1, width), jnp.float32)
+            final = (j, group) == (CL_DEV - 1, 1)
+            if final:
+
+                @pl.when(upper)
+                def _():
+                    def wait_lent(s, carry):
+                        lend(half + s, s, s).wait_recv()
+                        return carry
+
+                    lax.fori_loop(0, half, wait_lent, 0)
+                    k32 = lent[:, 0].reshape(span, width).astype(jnp.float32)
+                    vacant = k32 > 0.5 * EMPTY
+                    keys_x[...] = jnp.where(vacant, 0.0, k32).astype(jnp.bfloat16)
+                    flags = dot_t(ones, jnp.where(vacant, 1.0, 0.0).astype(jnp.bfloat16))
+                    bias_x[...] = jnp.where(flags > 0.5, LOW, 0.0)
+
             for b in range(zones):
                 first, last, far = group * half + b * part, group * half + (b + 1) * part, (b + 1) * block
 
@@ -304,13 +335,30 @@
                 scores = dot_t(q, keys[:far, :]) * scale + bias[0:1, :far]
                 tail = scores[:, b * block :] + causal
                 scores = tail if b == 0 else jnp.concatenate([scores[:, : b * block], tail], axis=1)
-                highest = jnp.max(scores, axis=1, keepdims=True)
-                weights = jnp.exp(scores - highest)
-                total = jnp.sum(weights, axis=1, keepdims=True)
                 v = recv[j, group * half : last, 2].reshape(far, width)
-                mixed = jnp.dot(weights.astype(jnp.bfloat16), v, preferred_element_type=jnp.float32)
-                att[j, first:last] = (mixed / total).astype(jnp.bfloat16).reshape(part, send, width)
-                parts[b * part : (b + 1) * part, j] = split(highest, total)
+
+                def finish(scores, v):
+                    highest = jnp.max(scores, axis=1, keepdims=True)
+                    weights = jnp.exp(scores - highest)
+                    total = jnp.sum(weights, axis=1, keepdims=True)
+                    mixed = jnp.dot(weights.astype(jnp.bfloat16), v, preferred_element_type=jnp.float32)
+                    att[j, first:last] = (mixed / total).astype(jnp.bfloat16).reshape(part, send, width)
+                    parts[b * part : (b + 1) * part, j] = split(highest, total)
+
+                if final:
+
+                    @pl.when(upper)
+                    def _():
+                        more = dot_t(q, keys_x[...]) * scale + bias_x[0:1, :]
+                        values = lent[:, 1].reshape(span, width)
+                        finish(jnp.concatenate([more, scores], axis=1), jnp.concatenate([values, v], axis=0))
+
+                    @pl.when(lower)
+                    def _():
+                        finish(scores, v)
+
+                else:
+                    finish(scores, v)
                 unit = unit_rows(q.astype(jnp.float32)) + unit_rows(k32)
                 sums = sums + jnp.sum(unit, axis=0, keepdims=True)
 
@@ -324,6 +372,8 @@
                 lax.fori_loop(first, last, give, 0)
             back[group * half + pos, j] = att[j, group * half + pos]
             held_sum[group, j : j + 1, :] = sums
+            if final:
+                continue
 
             @pl.when(lower)
             def _():
@@ -409,13 +459,15 @@
 
             @pl.when(upper)
             def _():
-                for j in range(CL_DEV):
+                for j in range(CL_DEV - group):
                     ask(j, d, group * half + pos, p).wait_send()
 
             @pl.when(lower)
             def _():
-                for j in range(CL_DEV):
+                for j in range(CL_DEV - group):
                     answered(j, d, group * half + pos, half + p).wait_send()
+                if group == 1:
+                    lend(d, pos, half + p).wait_send()
                 noted_x(d, group * half + pos, half + p).wait_send()
 
         return carry
@@ -493,6 +545,9 @@
             pltpu.VMEM((n, 1, 128), f32),
             pltpu.VMEM((n, 1, 128), f32),
             pltpu.VMEM((n, 1, 128), f32),
+            pltpu.VMEM((half, 2, send, width), bf16),
+            pltpu.VMEM((half * send, width), bf16),
+            pltpu.VMEM((8, half * send), f32),
             pltpu.VMEM((half * send, width), bf16),
             pltpu.VMEM((8, half * send), f32),
             pltpu.VMEM((tokens, 128), jnp.int32),

time: 56.8 us -> 56.6 us (level)
  no operation moved by 1% of the time
where the time goes in v4:
time: 56.6 us; the launch traced here: 56.4 us
  Pallas kernels  55.8 us (99%)
  between operations  0.64 us (1%)
    pallas_call x1, Pallas kernels, shards(): pl.pallas_call(functools.partial(kernel, n, heads, send), out_shape=(jax....  54.1 us
    pallas_call x1, Pallas kernels, project(): pl.pallas_call(functools.partial(project_kernel, steps), out_shape=(jax.S...  1.67 us

profile of v4, /device:TPU:16, one launch (start us, length us, event | category | flops | bytes accessed | tf_op | source)
XLA Modules:
  0.0 56.4 jit_solution(15830903444058714536)
XLA Ops:
  0.6 54.1 %route.1 = (bf16[1024,256]{1,0:T(8,128)(2,1)S(1)}, f32[2,128]{1,0:T(2,128)S(1)}, bf16[256,1024]{1,0:T(8,128)(2,1)S(1)}) custom-call(bf16[1,1024,128]{2,1,0:T(8,128)(2,1)} %q_hbm.1, bf16[1,1024,128]{2,1,0:T(8,128)(2,1)} %k_hbm.1, bf16[1,1024,128]{2,1,0:T(8,128)(2,1)} %v_hbm.1, s32[1,1024]{1,0:T(1,128)} %bitcast.1, bf16[256,1024]{1,0:T(8,128)(2,1)} %weight_hbm.1), custom_call_target="tpu_custom_call" | custom-call | tf_op jit(solution)/shard_map/route/pallas_call | solution.py:523
  54.7 1.7 %project.1 = (bf16[1024,1024]{1,0:T(8,128)(2,1)}, f32[1,2,128]{2,1,0:T(2,128)}) custom-call(bf16[1024,256]{1,0:T(8,128)(2,1)S(1)} %get-tuple-element.5.joined_ref, bf16[256,1024]{1,0:T(8,128)(2,1)S(1)} %get-tuple-element.6.weight_ref, f32[2,128]{1,0:T(2,128)S(1)} %get-tuple-element.7.sums_ref), custom_call_target="tpu_custom_call" | custom-call | tf_op jit(solution)/shard_map/project/pallas_call | solution.py:497
